TPU v7x, 32 devices: a whole 2x2x4 slice. The times are simulated.
32 devices in a mesh: groups: 2 (over x), row: 8 (over z, y), col: 2 (over core).
Axes of the slice: x: 2, y: 2, z: 4, core: 2. Of those that a mesh axis runs over, the one named last changes fastest.
Arguments:
- pair_repr: bfloat16 [64, 32, 128], P(('groups', 'row'), 'col'), parts along dimension 0, may hold values from -6 to 6
- in_gain: float32 [128], replicated, may hold values from 0.5 to 1.5
- in_bias: float32 [128], replicated, may hold values from -0.5 to 0.5
- left_gate_w: bfloat16 [128, 128], replicated, may hold values from -0.5 to 0.5
- left_w: bfloat16 [128, 128], replicated, may hold values from -0.5 to 0.5
- right_gate_w: bfloat16 [128, 128], replicated, may hold values from -0.5 to 0.5
- right_w: bfloat16 [128, 128], replicated, may hold values from -0.5 to 0.5
- out_gate_w: bfloat16 [128, 128], replicated, may hold values from -0.5 to 0.5
- mid_gain: float32 [128], replicated, may hold values from 0.5 to 1.5
- mid_bias: float32 [128], replicated, may hold values from -0.5 to 0.5
- out_w: bfloat16 [128, 128], replicated, may hold values from -0.5 to 0.5
Outputs:
- update: bfloat16 [64, 32, 128], P(('groups', 'row'), 'col'), parts along dimension 0
There are 2 independent parts, one for each index of `groups`. A program takes and returns all parts, laid end to end along the dimension named above; an argument that names none is the same for every part. Nothing has to cross between parts.
All inputs are finite; a program needn't handle non-finite values.
Results may differ from a plain program's by a relative error of at most 0.015.
Values may be sent and summed in bfloat16 or wider, within the bound.
A program may use at most 64 MiB of HBM per device.

v0:
```python
import jax
import jax.numpy as jnp
from jax import lax
from jax.sharding import PartitionSpec as P


def layer_norm(values, norm_gain, norm_bias):
    average = jnp.mean(values, axis=-1, keepdims=True)
    centred = values - average
    variance = jnp.mean(centred * centred, axis=-1, keepdims=True)
    return centred / jnp.sqrt(variance + 1e-05) * norm_gain + norm_bias


def on_device(
    pair_repr,
    in_gain,
    in_bias,
    left_gate_w,
    left_w,
    right_gate_w,
    right_w,
    out_gate_w,
    mid_gain,
    mid_bias,
    out_w,
):
    row_count, col_count, channels = pair_repr.shape
    hidden = left_w.shape[1]
    normed = layer_norm(pair_repr.astype(jnp.float32), in_gain, in_bias).astype(jnp.bfloat16)
    flattened = normed.reshape(row_count * col_count, channels)
    left_side = (
        (
            jax.nn.sigmoid(jnp.dot(flattened, left_gate_w, preferred_element_type=jnp.float32))
            * jnp.dot(flattened, left_w, preferred_element_type=jnp.float32)
        )
        .astype(jnp.bfloat16)
        .reshape(row_count, col_count, hidden)
    )
    right_side = (
        (
            jax.nn.sigmoid(jnp.dot(flattened, right_gate_w, preferred_element_type=jnp.float32))
            * jnp.dot(flattened, right_w, preferred_element_type=jnp.float32)
        )
        .astype(jnp.bfloat16)
        .reshape(row_count, col_count, hidden)
    )
    gating = jax.nn.sigmoid(jnp.dot(flattened, out_gate_w, preferred_element_type=jnp.float32))
    left_full = lax.all_gather(left_side, "col", axis=1, tiled=True)
    right_all = lax.all_gather(right_side, "row", axis=0, tiled=True)
    right_mine = lax.all_to_all(right_all, "col", split_axis=0, concat_axis=1, tiled=True)
    triangle = jnp.einsum("ikh,jkh->ijh", left_full, right_mine, preferred_element_type=jnp.float32)
    middle = (
        layer_norm(triangle, mid_gain, mid_bias)
        .astype(jnp.bfloat16)
        .reshape(row_count * col_count, hidden)
    )
    result = gating * jnp.dot(middle, out_w, preferred_element_type=jnp.float32)
    return result.astype(jnp.bfloat16).reshape(row_count, col_count, channels)


def solution(mesh):
    in_specs = (P(("groups", "row"), "col", None), P(), P(), P(), P(), P(), P(), P(), P(), P(), P())
    out_specs = P(("groups", "row"), "col", None)
    return jax.shard_map(
        on_device, mesh=mesh, in_specs=in_specs, out_specs=out_specs, check_vma=False
    )
```

profile of v0, /device:TPU:0, one launch (start us, length us, event | category | flops | bytes accessed | tf_op | source)
XLA Modules:
  0.0 45.9 jit_solution(8318891046903231604)
XLA Ops:
  0.0 0.0 copy-start
  0.0 0.9 %convert_reduce_fusion = f32[4,16]{1,0:T(4,128)S(1)} fusion(bf16[4,16,128]{2,1,0:T(8,128)(2,1)} %param.11), kind=kLoop, calls=%fused_computation.19 | loop fusion | flops 16320 | bytes 16640 | tf_op jit(solution)/shard_map/reduce_sum | solution.py:8
  0.9 0.0 copy-done.1
  0.9 0.2 fusion.14
  1.1 0.6 %copy-done.5 = f32[128]{0:T(128)S(1)} copy-done((f32[128]{0:T(128)S(1)}, f32[128]{0:T(128)}, u32[]{:S(2)}) %copy-start.5) | copy-done | bytes 536
  1.7 0.0 copy-done.6
  1.7 0.1 fusion.17
  1.8 0.0 copy-start.2
  1.8 0.1 fusion.5
  2.0 0.6 %copy-done.2 = bf16[128,128]{1,0:T(8,128)(2,1)S(1)} copy-done((bf16[128,128]{1,0:T(8,128)(2,1)S(1)}, bf16[128,128]{1,0:T(8,128)(2,1)}, u32[]{:S(2)}) %copy-start.2) | copy-done | bytes 32792
  2.6 0.1 fusion.9
  2.7 32.3 %all_gather.6 = bf16[32,16,128]{2,1,0:T(8,128)(2,1)S(1)} all-gather(bf16[4,16,128]{2,1,0:T(8,128)(2,1)S(1)} %bitcast.37), channel_id=1, replica_groups=mesh['groups'=2,'row'=8,'col'=2] {'row'}, dimensions={0}, use_global_device_ids=true | all-gather | bytes 147456 | tf_op jit(solution)/shard_map/all_gather | solution.py:49
  35.0 3.8 %all_to_all.18 = bf16[32,16,128]{2,1,0:T(8,128)(2,1)S(1)} all-to-all(bf16[32,16,128]{2,1,0:T(8,128)(2,1)S(1)} %all_gather.6), channel_id=1, replica_groups=mesh['groups'=2,'row'=8,'col'=2] {'col'}, dimensions={0} | all-to-all | bytes 262144 | tf_op jit(solution)/shard_map/all_to_all | solution.py:50
  38.9 0.0 copy-start.9
  38.9 0.4 copy.28
  39.3 0.3 copy-done.9
  39.6 0.1 fusion.2
  39.8 0.6 %copy-done.3 = bf16[128,128]{1,0:T(8,128)(2,1)S(1)} copy-done((bf16[128,128]{1,0:T(8,128)(2,1)S(1)}, bf16[128,128]{1,0:T(8,128)(2,1)}, u32[]{:S(2)}) %copy-start.3) | copy-done | bytes 32792
  40.4 0.1 fusion.10
  40.5 1.8 %all_gather.7 = bf16[4,32,128]{2,0,1:T(4,128)(2,1)S(1)} all-gather(bf16[4,16,128]{2,0,1:T(4,128)(2,1)S(1)} %copy.27), channel_id=1, replica_groups=mesh['groups'=2,'row'=8,'col'=2] {'col'}, dimensions={1}, use_global_device_ids=true | all-gather | bytes 49152 | tf_op jit(solution)/shard_map/all_gather | solution.py:48
  42.4 0.1 copy.29
  42.5 0.4 fusion.18
  42.9 0.1 copy.30
  43.0 0.1 bitcast_reduce_fusion
  43.1 0.2 multiply_reduce_fusion
  43.3 0.5 %copy-done.10 = bf16[128,128]{1,0:T(8,128)(2,1)S(1)} copy-done((bf16[128,128]{1,0:T(8,128)(2,1)S(1)}, bf16[128,128]{1,0:T(8,128)(2,1)}, u32[]{:S(2)}) %copy-start.10) | copy-done | bytes 32792
  43.8 0.1 fusion.8
  43.9 0.5 %copy-done.7 = f32[128]{0:T(128)S(1)} copy-done((f32[128]{0:T(128)S(1)}, f32[128]{0:T(128)}, u32[]{:S(2)}) %copy-start.7) | copy-done | bytes 536
  44.4 0.0 copy-done.8
  44.4 0.1 add_convert_fusion
  44.5 0.7 %copy-done.4 = bf16[128,128]{1,0:T(8,128)(2,1)S(1)} copy-done((bf16[128,128]{1,0:T(8,128)(2,1)S(1)}, bf16[128,128]{1,0:T(8,128)(2,1)}, u32[]{:S(2)}) %copy-start.4) | copy-done | bytes 32792
  45.2 0.7 %fusion.11 = bf16[64,128]{1,0:T(8,128)(2,1)} fusion(f32[64,128]{1,0:T(8,128)S(1)} %fusion.8, bf16[64,128]{1,0:T(8,128)(2,1)S(1)} %bitcast.38, bf16[128,128]{1,0:T(8,128)(2,1)S(1)} %copy-done.4), kind=kOutput, calls=%fused_computation.17 | convolution fusion | flops 2113536 | bytes 98304 | tf_op jit(solution)/shard_map/dot_general | solution.py:57
  (15 shorter events, 0.1 us)
Async XLA Ops:
  0.0 1.8 %copy-start = (bf16[128,128]{1,0:T(8,128)(2,1)S(1)}, bf16[128,128]{1,0:T(8,128)(2,1)}, u32[]{:S(2)}) copy-start(bf16[128,128]{1,0:T(8,128)(2,1)} %param.16) | copy-start | bytes 98308
  0.0 0.9 %copy-start.1 = (bf16[4,16,128]{2,1,0:T(8,128)(2,1)S(1)}, bf16[4,16,128]{2,1,0:T(8,128)(2,1)}, u32[]{:S(2)}) copy-start(bf16[4,16,128]{2,1,0:T(8,128)(2,1)} %param.11) | copy-start | bytes 49156
  1.0 0.7 %copy-start.5 = (f32[128]{0:T(128)S(1)}, f32[128]{0:T(128)}, u32[]{:S(2)}) copy-start(f32[128]{0:T(128)} %param.13) | copy-start | bytes 1540
  1.1 0.7 %copy-start.6 = (f32[128]{0:T(128)S(1)}, f32[128]{0:T(128)}, u32[]{:S(2)}) copy-start(f32[128]{0:T(128)} %param.12) | copy-start | bytes 1540
  1.8 0.8 %copy-start.2 = (bf16[128,128]{1,0:T(8,128)(2,1)S(1)}, bf16[128,128]{1,0:T(8,128)(2,1)}, u32[]{:S(2)}) copy-start(bf16[128,128]{1,0:T(8,128)(2,1)} %param.17) | copy-start | bytes 98308
  38.9 0.8 %copy-start.9 = (bf16[128,128]{1,0:T(8,128)(2,1)S(1)}, bf16[128,128]{1,0:T(8,128)(2,1)}, u32[]{:S(2)}) copy-start(bf16[128,128]{1,0:T(8,128)(2,1)} %param.14) | copy-start | bytes 98308
  39.6 0.8 %copy-start.3 = (bf16[128,128]{1,0:T(8,128)(2,1)S(1)}, bf16[128,128]{1,0:T(8,128)(2,1)}, u32[]{:S(2)}) copy-start(bf16[128,128]{1,0:T(8,128)(2,1)} %param.15) | copy-start | bytes 98308
  43.0 0.8 %copy-start.10 = (bf16[128,128]{1,0:T(8,128)(2,1)S(1)}, bf16[128,128]{1,0:T(8,128)(2,1)}, u32[]{:S(2)}) copy-start(bf16[128,128]{1,0:T(8,128)(2,1)} %param.18) | copy-start | bytes 98308
  43.8 0.7 %copy-start.7 = (f32[128]{0:T(128)S(1)}, f32[128]{0:T(128)}, u32[]{:S(2)}) copy-start(f32[128]{0:T(128)} %param.20) | copy-start | bytes 1540
  43.8 0.7 %copy-start.8 = (f32[128]{0:T(128)S(1)}, f32[128]{0:T(128)}, u32[]{:S(2)}) copy-start(f32[128]{0:T(128)} %param.19) | copy-start | bytes 1540
  44.4 0.8 %copy-start.4 = (bf16[128,128]{1,0:T(8,128)(2,1)S(1)}, bf16[128,128]{1,0:T(8,128)(2,1)}, u32[]{:S(2)}) copy-start(bf16[128,128]{1,0:T(8,128)(2,1)} %param.21) | copy-start | bytes 98308
where the time goes:
time: 46.5 us; the launch traced here: 45.9 us
  blocking collectives  38 us (82%)
  local copies, waits for them, and re-layouts  4.56 us (10%)
  matrix products  1.79 us (4%)
  other arithmetic  1.48 us (3%)
    all_gather x1, blocking collectives, on_device(): right_all = lax.all_gather(right_side, 'row', axis=0, tiled=True)  32.3 us
    unnamed x22, local copies, waits for them, and re-layouts  3.86 us
    all_to_all x1, blocking collectives, on_device(): lax.all_to_all(right_all, 'col', split_axis=0, concat_axis=1, tiled=True)  3.83 us
    all_gather x1, blocking collectives, on_device(): left_full = lax.all_gather(left_side, 'col', axis=1, tiled=True)  1.83 us
    reduce_sum x2, other arithmetic, layer_norm(): average = jnp.mean(values, axis=-1, keepdims=True)  0.96 us

commit v1 on v0

--- a/solution.py
+++ b/solution.py
@@ -2,6 +2,19 @@
 import jax.numpy as jnp
 from jax import lax
 from jax.sharding import PartitionSpec as P
+
+
+def handle_block(content):
+    chip_axis = "row"
+    sides = lax.axis_size(chip_axis)
+    gallery = [content]
+    for tick in range(sides - 1):
+        val = lax.ppermute(
+            gallery[-1], chip_axis, perm=[(rr, (rr + 1) % sides) for rr in range(sides)]
+        )
+        gallery.append(val)
+    now = jnp.concatenate(gallery[::-1], 0)
+    return jnp.roll(now, (lax.axis_index(chip_axis) + 1) * content.shape[0], axis=0)
 
 
 def layer_norm(values, norm_gain, norm_bias):
@@ -46,7 +59,7 @@
     )
     gating = jax.nn.sigmoid(jnp.dot(flattened, out_gate_w, preferred_element_type=jnp.float32))
     left_full = lax.all_gather(left_side, "col", axis=1, tiled=True)
-    right_all = lax.all_gather(right_side, "row", axis=0, tiled=True)
+    right_all = handle_block(right_side)
     right_mine = lax.all_to_all(right_all, "col", split_axis=0, concat_axis=1, tiled=True)
     triangle = jnp.einsum("ikh,jkh->ijh", left_full, right_mine, preferred_element_type=jnp.float32)
     middle = (

time: 46.5 us -> 56.2 us (1.21)
  waiting for transfers between devices: 0 us -> 40.9 us
  blocking collectives: 38 us -> 5.67 us
  starting transfers between devices: 0 us -> 2.99 us
  local copies, waits for them, and re-layouts: 4.56 us -> 2.8 us
    ppermute x0 -> x7, waiting for transfers between devices: none -> 40.9 us  [handle_block(): lax.ppermute(gallery[-1], chip_axis, perm=[(rr, (rr + 1) % sides) for rr...]
    all_gather x1 -> x0, blocking collectives: 32.3 us -> none  [on_device(): right_all = lax.all_gather(right_side, 'row', axis=0, tiled=True)]
    ppermute x0 -> x7, starting transfers between devices: none -> 2.99 us  [handle_block(): lax.ppermute(gallery[-1], chip_axis, perm=[(rr, (rr + 1) % sides) for rr...]
    unnamed x22 -> x37, local copies, waits for them, and re-layouts: 3.86 us -> 2.07 us
  transfers between devices with their start and end apart: 0 -> 7, of which waited for: 0 -> 7; matrix products, arithmetic and copies ran while one was open for 0% -> 1% of each run, Pallas kernels for 0% -> 0%
where the time goes in v1:
time: 56.2 us; the launch traced here: 55.9 us
  waiting for transfers between devices  40.9 us (73%)
  blocking collectives  5.67 us (10%)
  starting transfers between devices  2.99 us (5%)
  local copies, waits for them, and re-layouts  2.8 us (5%)
  matrix products  1.8 us (3%)
  other arithmetic  1.49 us (3%)
    ppermute x7, waiting for transfers between devices, handle_block(): lax.ppermute(gallery[-1], chip_axis, perm=[(rr, (rr + 1) % sides) for rr...  40.9 us
    all_to_all x1, blocking collectives, on_device(): lax.all_to_all(right_all, 'col', split_axis=0, concat_axis=1, tiled=True)  3.84 us
    ppermute x7, starting transfers between devices, handle_block(): lax.ppermute(gallery[-1], chip_axis, perm=[(rr, (rr + 1) % sides) for rr...  2.99 us
    unnamed x37, local copies, waits for them, and re-layouts  2.07 us
    all_gather x1, blocking collectives, on_device(): left_full = lax.all_gather(left_side, 'col', axis=1, tiled=True)  1.83 us
  transfers between devices with their start and end apart: 7, of which 7 were waited for; matrix products, arithmetic and copies ran while one was open for 1% of the time, Pallas kernels for 0%

profile of v1, /device:TPU:0, one launch (start us, length us, event | category | flops | bytes accessed | tf_op | source)
XLA Modules:
  0.0 55.9 jit_solution(16911057987291468324)
XLA Ops:
  0.0 0.9 %convert_reduce_fusion = f32[4,16]{1,0:T(4,128)S(1)} fusion(bf16[4,16,128]{2,1,0:T(8,128)(2,1)} %param.11), kind=kLoop, calls=%fused_computation.19 | loop fusion | flops 16320 | bytes 16640 | tf_op jit(solution)/shard_map/reduce_sum | solution.py:21
  0.9 0.2 fusion.14
  1.1 0.6 %copy-done.5 = f32[128]{0:T(128)S(1)} copy-done((f32[128]{0:T(128)S(1)}, f32[128]{0:T(128)}, u32[]{:S(2)}) %copy-start.5) | copy-done | bytes 536
  1.7 0.0 copy-done.6
  1.7 0.1 fusion.17
  1.8 0.1 fusion.5
  2.0 0.6 %copy-done.2 = bf16[128,128]{1,0:T(8,128)(2,1)S(1)} copy-done((bf16[128,128]{1,0:T(8,128)(2,1)S(1)}, bf16[128,128]{1,0:T(8,128)(2,1)}, u32[]{:S(2)}) %copy-start.2) | copy-done | bytes 32792
  2.6 0.1 fusion.9
  2.7 3.0 %collective-permute-start = (bf16[4,16,128]{2,1,0:T(8,128)(2,1)S(1)}, bf16[4,16,128]{2,1,0:T(8,128)(2,1)S(1)}, u32[]{:S(2)}, u32[]{:S(2)}) collective-permute-start(bf16[4,16,128]{2,1,0:T(8,128)(2,1)S(1)} %bitcast.32), channel_id=1, source_target_pairs={{0,2},{2,4},{4,6},{6,8},{8,10},{10,12},{12,14},{14,0},{1,3},{3,5},... | collective-permute-start | bytes 49160 | tf_op jit(solution)/shard_map/ppermute | solution.py:12
  5.7 4.8 %collective-permute-done = bf16[4,16,128]{2,1,0:T(8,128)(2,1)S(1)} collective-permute-done((bf16[4,16,128]{2,1,0:T(8,128)(2,1)S(1)}, bf16[4,16,128]{2,1,0:T(8,128)(2,1)S(1)}, u32[]{:S(2)}, u32[]{:S(2)}) %collective-permute-start) | collective-permute-done | bytes 16416 | tf_op jit(solution)/shard_map/ppermute | solution.py:12
  10.5 6.4 %collective-permute-done.1 = bf16[4,16,128]{2,1,0:T(8,128)(2,1)S(1)} collective-permute-done((bf16[4,16,128]{2,1,0:T(8,128)(2,1)S(1)}, bf16[4,16,128]{2,1,0:T(8,128)(2,1)S(1)}, u32[]{:S(2)}, u32[]{:S(2)}) %collective-permute-start.1) | collective-permute-done | bytes 16416 | tf_op jit(solution)/shard_map/ppermute | solution.py:12
  16.9 6.4 %collective-permute-done.2 = bf16[4,16,128]{2,1,0:T(8,128)(2,1)S(1)} collective-permute-done((bf16[4,16,128]{2,1,0:T(8,128)(2,1)S(1)}, bf16[4,16,128]{2,1,0:T(8,128)(2,1)S(1)}, u32[]{:S(2)}, u32[]{:S(2)}) %collective-permute-start.2) | collective-permute-done | bytes 16416 | tf_op jit(solution)/shard_map/ppermute | solution.py:12
  23.3 6.4 %collective-permute-done.3 = bf16[4,16,128]{2,1,0:T(8,128)(2,1)S(1)} collective-permute-done((bf16[4,16,128]{2,1,0:T(8,128)(2,1)S(1)}, bf16[4,16,128]{2,1,0:T(8,128)(2,1)S(1)}, u32[]{:S(2)}, u32[]{:S(2)}) %collective-permute-start.3) | collective-permute-done | bytes 16416 | tf_op jit(solution)/shard_map/ppermute | solution.py:12
  29.8 0.1 fusion.2
  29.9 6.3 %collective-permute-done.4 = bf16[4,16,128]{2,1,0:T(8,128)(2,1)S(1)} collective-permute-done((bf16[4,16,128]{2,1,0:T(8,128)(2,1)S(1)}, bf16[4,16,128]{2,1,0:T(8,128)(2,1)S(1)}, u32[]{:S(2)}, u32[]{:S(2)}) %collective-permute-start.4) | collective-permute-done | bytes 16416 | tf_op jit(solution)/shard_map/ppermute | solution.py:12
  36.2 0.1 fusion.10
  36.3 6.3 %collective-permute-done.5 = bf16[4,16,128]{2,1,0:T(8,128)(2,1)S(1)} collective-permute-done((bf16[4,16,128]{2,1,0:T(8,128)(2,1)S(1)}, bf16[4,16,128]{2,1,0:T(8,128)(2,1)S(1)}, u32[]{:S(2)}, u32[]{:S(2)}) %collective-permute-start.5) | collective-permute-done | bytes 16416 | tf_op jit(solution)/shard_map/ppermute | solution.py:12
  42.7 0.1 fusion.8
  42.8 1.8 %all_gather.3 = bf16[4,32,128]{2,0,1:T(4,128)(2,1)S(1)} all-gather(bf16[4,16,128]{2,0,1:T(4,128)(2,1)S(1)} %copy.27), channel_id=1, replica_groups=mesh['groups'=2,'row'=8,'col'=2] {'col'}, dimensions={1}, use_global_device_ids=true | all-gather | bytes 49152 | tf_op jit(solution)/shard_map/all_gather | solution.py:61
  44.7 0.1 copy.29
  44.8 4.3 %collective-permute-done.6 = bf16[4,16,128]{2,1,0:T(8,128)(2,1)S(1)} collective-permute-done((bf16[4,16,128]{2,1,0:T(8,128)(2,1)S(1)}, bf16[4,16,128]{2,1,0:T(8,128)(2,1)S(1)}, u32[]{:S(2)}, u32[]{:S(2)}) %collective-permute-start.6) | collective-permute-done | bytes 16416 | tf_op jit(solution)/shard_map/ppermute | solution.py:12
  49.3 3.8 %all_to_all.18 = bf16[32,16,128]{2,1,0:T(8,128)(2,1)S(1)} all-to-all(bf16[32,16,128]{2,1,0:T(8,128)(2,1)S(1)} %constant_dynamic-slice_fusion), channel_id=1, replica_groups=mesh['groups'=2,'row'=8,'col'=2] {'col'}, dimensions={0} | all-to-all | bytes 262144 | tf_op jit(solution)/shard_map/all_to_all | solution.py:63
  53.1 0.4 copy.28
  53.6 0.4 fusion.18
  53.9 0.1 copy.30
  54.1 0.1 bitcast_reduce_fusion
  54.2 0.2 multiply_reduce_fusion
  54.4 0.4 copy-done.7
  54.7 0.0 copy-done.8
  54.8 0.1 add_convert_fusion
  54.8 0.3 copy-done.4
  55.1 0.7 %fusion.11 = bf16[64,128]{1,0:T(8,128)(2,1)} fusion(f32[64,128]{1,0:T(8,128)S(1)} %fusion.8, bf16[64,128]{1,0:T(8,128)(2,1)S(1)} %bitcast.41, bf16[128,128]{1,0:T(8,128)(2,1)S(1)} %copy-done.4), kind=kOutput, calls=%fused_computation.17 | convolution fusion | flops 2113536 | bytes 98304 | tf_op jit(solution)/shard_map/dot_general | solution.py:70
  (45 shorter events, 0.3 us)
Async XLA Ops:
  0.0 1.8 %copy-start = (bf16[128,128]{1,0:T(8,128)(2,1)S(1)}, bf16[128,128]{1,0:T(8,128)(2,1)}, u32[]{:S(2)}) copy-start(bf16[128,128]{1,0:T(8,128)(2,1)} %param.16) | copy-start | bytes 98308
  0.0 0.9 %copy-start.1 = (bf16[4,16,128]{2,1,0:T(8,128)(2,1)S(1)}, bf16[4,16,128]{2,1,0:T(8,128)(2,1)}, u32[]{:S(2)}) copy-start(bf16[4,16,128]{2,1,0:T(8,128)(2,1)} %param.11) | copy-start | bytes 49156
  1.0 0.7 %copy-start.5 = (f32[128]{0:T(128)S(1)}, f32[128]{0:T(128)}, u32[]{:S(2)}) copy-start(f32[128]{0:T(128)} %param.13) | copy-start | bytes 1540
  1.1 0.7 %copy-start.6 = (f32[128]{0:T(128)S(1)}, f32[128]{0:T(128)}, u32[]{:S(2)}) copy-start(f32[128]{0:T(128)} %param.12) | copy-start | bytes 1540
  1.8 0.8 %copy-start.2 = (bf16[128,128]{1,0:T(8,128)(2,1)S(1)}, bf16[128,128]{1,0:T(8,128)(2,1)}, u32[]{:S(2)}) copy-start(bf16[128,128]{1,0:T(8,128)(2,1)} %param.17) | copy-start | bytes 98308
  2.6 27.2 %copy-start.9 = (bf16[128,128]{1,0:T(8,128)(2,1)S(1)}, bf16[128,128]{1,0:T(8,128)(2,1)}, u32[]{:S(2)}) copy-start(bf16[128,128]{1,0:T(8,128)(2,1)} %param.14) | copy-start | bytes 98308
  2.7 33.5 %copy-start.3 = (bf16[128,128]{1,0:T(8,128)(2,1)S(1)}, bf16[128,128]{1,0:T(8,128)(2,1)}, u32[]{:S(2)}) copy-start(bf16[128,128]{1,0:T(8,128)(2,1)} %param.15) | copy-start | bytes 98308
  2.7 7.7 %collective-permute-start = (bf16[4,16,128]{2,1,0:T(8,128)(2,1)S(1)}, bf16[4,16,128]{2,1,0:T(8,128)(2,1)S(1)}, u32[]{:S(2)}, u32[]{:S(2)}) collective-permute-start(bf16[4,16,128]{2,1,0:T(8,128)(2,1)S(1)} %bitcast.32), channel_id=1, source_target_pairs={{0,2},{2,4},{4,6},{6,8},{8,10},{10,12},{12,14},{14,0},{1,3},{3,5},... | collective-permute-start | bytes 49160 | tf_op jit(solution)/shard_map/ppermute | solution.py:12
  10.5 6.4 %collective-permute-start.1 = (bf16[4,16,128]{2,1,0:T(8,128)(2,1)S(1)}, bf16[4,16,128]{2,1,0:T(8,128)(2,1)S(1)}, u32[]{:S(2)}, u32[]{:S(2)}) collective-permute-start(bf16[4,16,128]{2,1,0:T(8,128)(2,1)S(1)} %collective-permute-done), channel_id=1, source_target_pairs={{0,2},{2,4},{4,6},{6,8},{8,10},{10,12},{12,14},{14,0},{1,3},{3,5},... | collective-permute-start | bytes 49160 | tf_op jit(solution)/shard_map/ppermute | solution.py:12
  16.9 6.4 %collective-permute-start.2 = (bf16[4,16,128]{2,1,0:T(8,128)(2,1)S(1)}, bf16[4,16,128]{2,1,0:T(8,128)(2,1)S(1)}, u32[]{:S(2)}, u32[]{:S(2)}) collective-permute-start(bf16[4,16,128]{2,1,0:T(8,128)(2,1)S(1)} %collective-permute-done.1), channel_id=1, source_target_pairs={{0,2},{2,4},{4,6},{6,8},{8,10},{10,12},{12,14},{14,0},{1,3},{3,5},... | collective-permute-start | bytes 49160 | tf_op jit(solution)/shard_map/ppermute | solution.py:12
  23.3 6.4 %collective-permute-start.3 = (bf16[4,16,128]{2,1,0:T(8,128)(2,1)S(1)}, bf16[4,16,128]{2,1,0:T(8,128)(2,1)S(1)}, u32[]{:S(2)}, u32[]{:S(2)}) collective-permute-start(bf16[4,16,128]{2,1,0:T(8,128)(2,1)S(1)} %collective-permute-done.2), channel_id=1, source_target_pairs={{0,2},{2,4},{4,6},{6,8},{8,10},{10,12},{12,14},{14,0},{1,3},{3,5},... | collective-permute-start | bytes 49160 | tf_op jit(solution)/shard_map/ppermute | solution.py:12
  29.8 6.4 %collective-permute-start.4 = (bf16[4,16,128]{2,1,0:T(8,128)(2,1)S(1)}, bf16[4,16,128]{2,1,0:T(8,128)(2,1)S(1)}, u32[]{:S(2)}, u32[]{:S(2)}) collective-permute-start(bf16[4,16,128]{2,1,0:T(8,128)(2,1)S(1)} %collective-permute-done.3), channel_id=1, source_target_pairs={{0,2},{2,4},{4,6},{6,8},{8,10},{10,12},{12,14},{14,0},{1,3},{3,5},... | collective-permute-start | bytes 49160 | tf_op jit(solution)/shard_map/ppermute | solution.py:12
  29.9 12.7 %copy-start.10 = (bf16[128,128]{1,0:T(8,128)(2,1)S(1)}, bf16[128,128]{1,0:T(8,128)(2,1)}, u32[]{:S(2)}) copy-start(bf16[128,128]{1,0:T(8,128)(2,1)} %param.18) | copy-start | bytes 98308
  36.2 6.4 %collective-permute-start.5 = (bf16[4,16,128]{2,1,0:T(8,128)(2,1)S(1)}, bf16[4,16,128]{2,1,0:T(8,128)(2,1)S(1)}, u32[]{:S(2)}, u32[]{:S(2)}) collective-permute-start(bf16[4,16,128]{2,1,0:T(8,128)(2,1)S(1)} %collective-permute-done.4), channel_id=1, source_target_pairs={{0,2},{2,4},{4,6},{6,8},{8,10},{10,12},{12,14},{14,0},{1,3},{3,5},... | collective-permute-start | bytes 49160 | tf_op jit(solution)/shard_map/ppermute | solution.py:12
  42.6 6.4 %collective-permute-start.6 = (bf16[4,16,128]{2,1,0:T(8,128)(2,1)S(1)}, bf16[4,16,128]{2,1,0:T(8,128)(2,1)S(1)}, u32[]{:S(2)}, u32[]{:S(2)}) collective-permute-start(bf16[4,16,128]{2,1,0:T(8,128)(2,1)S(1)} %collective-permute-done.5), channel_id=1, source_target_pairs={{0,2},{2,4},{4,6},{6,8},{8,10},{10,12},{12,14},{14,0},{1,3},{3,5},... | collective-permute-start | bytes 49160 | tf_op jit(solution)/shard_map/ppermute | solution.py:12
  54.1 0.7 %copy-start.7 = (f32[128]{0:T(128)S(1)}, f32[128]{0:T(128)}, u32[]{:S(2)}) copy-start(f32[128]{0:T(128)} %param.20) | copy-start | bytes 1540
  54.1 0.7 %copy-start.8 = (f32[128]{0:T(128)S(1)}, f32[128]{0:T(128)}, u32[]{:S(2)}) copy-start(f32[128]{0:T(128)} %param.19) | copy-start | bytes 1540
  54.3 0.8 %copy-start.4 = (bf16[128,128]{1,0:T(8,128)(2,1)S(1)}, bf16[128,128]{1,0:T(8,128)(2,1)}, u32[]{:S(2)}) copy-start(bf16[128,128]{1,0:T(8,128)(2,1)} %param.21) | copy-start | bytes 98308
